TPU v7x, 32 devices: a whole 2x2x4 slice. The times are simulated.
32 devices in a mesh: row: 4 (over y, x), col: 8 (over z, core).
Axes of the slice: x: 2, y: 2, z: 4, core: 2. Of those that a mesh axis runs over, the one named last changes fastest.
Arguments:
- trailing_slab: bfloat16 [24576, 8192], P('row', 'col'), may hold values from -6 to 6
- panel_cols: bfloat16 [24576, 512], P('row', 'col'), may hold values from -0.25 to 0.25
- head_slab: bfloat16 [512, 8192], P('row', 'col'), may hold values from -6 to 6
- coupling: bfloat16 [2, 256, 256], replicated, may hold values from -0.25 to 0.25
- lower_inverses: bfloat16 [2, 256, 256], replicated, may hold values from -1.5 to 1.5, as said below
- upper_inverses: bfloat16 [2, 256, 256], replicated, may hold values from -1.5 to 1.5, as said below
Outputs:
- trailing: bfloat16 [24576, 8192], P('row', 'col')
Inputs may be any that keep to these rules, and one draw needn't show every extreme that they name: `lower_inverses`: each of the two [256, 256] blocks is lower triangular with unit diagonal. `upper_inverses`: each of the two [256, 256] blocks is upper triangular with diagonal between 0.5 and 1.5.
All inputs are finite; a program needn't handle non-finite values.
Results may differ from a plain program's by a relative error of at most 0.0067.
Values may be sent and summed in bfloat16 or wider, within the bound.
No kernel may reach another device: no remote copies, remote signals or barrier semaphores. Data moves between devices by JAX's collectives and lax.ppermute only.
A program may use at most 128 MiB of HBM per device.

v0:
```python
import jax
import jax.numpy as jnp
from jax import lax
from jax.sharding import PartitionSpec as P


def product(left, right):
    return jnp.dot(left, right, preferred_element_type=jnp.float32)


def factor_panel(panel_block, upper_mid, upper_inverses):
    width = upper_mid.shape[0]
    lower_first = product(panel_block[:, :width], upper_inverses[0]).astype(jnp.bfloat16)
    panel_second = (
        panel_block[:, width:].astype(jnp.float32) - product(lower_first, upper_mid)
    ).astype(jnp.bfloat16)
    lower_second = product(panel_second, upper_inverses[1]).astype(jnp.bfloat16)
    return jnp.concatenate([lower_first, lower_second], axis=1)


def apply_update(slab_part, lower_block, upper_both):
    result = slab_part.astype(jnp.float32) - product(lower_block, upper_both)
    return result.astype(jnp.bfloat16)


def on_device(trailing_slab, panel_cols, head_slab, coupling, lower_inverses, upper_inverses):
    width = coupling.shape[1]
    head_full = lax.all_gather(head_slab, "row", axis=0, tiled=True)
    upper_mid = product(lower_inverses[0], coupling[0]).astype(jnp.bfloat16)
    upper_first = product(lower_inverses[0], head_full[:width]).astype(jnp.bfloat16)
    lower_head = product(coupling[1], upper_inverses[0]).astype(jnp.bfloat16)
    head_second = (head_full[width:].astype(jnp.float32) - product(lower_head, upper_first)).astype(
        jnp.bfloat16
    )
    upper_second = product(lower_inverses[1], head_second).astype(jnp.bfloat16)
    upper_both = jnp.concatenate([upper_first, upper_second], axis=0)
    panel_full = lax.all_gather(panel_cols, "col", axis=1, tiled=True)
    lower_block = factor_panel(panel_full, upper_mid, upper_inverses)
    return apply_update(trailing_slab, lower_block, upper_both)


def solution(mesh):
    in_specs = (P("row", "col"), P("row", "col"), P("row", "col"), P(), P(), P())
    out_specs = P("row", "col")
    return jax.shard_map(
        on_device, mesh=mesh, in_specs=in_specs, out_specs=out_specs, check_vma=False
    )
```

profile of v0, /device:TPU:0, one launch (start us, length us, event | category | flops | bytes accessed | tf_op | source)
XLA Modules:
  0.0 133.2 jit_solution(17150895435019928692)
XLA Ops:
  6.5 0.0 all-gather.5.cloned.1.call-start
  6.5 0.7 all-gather.5.cloned.1.call-update
  7.3 0.0 all-gather.3.cloned.1.call-start
  7.3 0.7 all-gather.3.cloned.1.call-update
  8.0 1.2 convolution_convert_fusion.4
  9.2 1.2 convolution_convert_fusion.5
  10.3 0.0 copy-start.1
  10.3 28.1 %all-gather.5.cloned.1.call-done = bf16[512,1024]{1,0:T(8,128)(2,1)} async-done(((bf16[128,1024]{1,0:T(8,128)(2,1)}), bf16[512,1024]{1,0:T(8,128)(2,1)}) %all-gather.5.cloned.1.call-update) | async-done | bytes 1048592 | tf_op jit(solution)/shard_map/all_gather | solution.py:28
  38.4 1.4 %convolution_convert_fusion.3 = bf16[256,1024]{1,0:T(8,128)(2,1)S(1)} fusion(bf16[512,1024]{1,0:T(8,128)(2,1)} %all-gather.5.cloned.1.call-done, bf16[2,256,256]{2,1,0:T(8,128)(2,1)} %param.10), kind=kOutput, calls=%fused_computation.11 | convolution fusion | flops 134479872 | bytes 1179648 | tf_op jit(solution)/shard_map/dot_general | solution.py:8
  39.9 0.0 copy-start
  39.9 2.6 %fusion.6 = bf16[256,1024]{1,0:T(8,128)(2,1)} fusion(bf16[256,256]{1,0:T(8,128)(2,1)S(1)} %convolution_convert_fusion.4, bf16[256,1024]{1,0:T(8,128)(2,1)S(1)} %convolution_convert_fusion.3, bf16[512,1024]{1,0:T(8,128)(2,1)} %all-gather.5.cloned.1.call-done, bf16[2,256,256]{2,1,0:T(8,128)(2,1)} %param.10), kind=kOutput, calls=%fused_computation.13 | convolution fusion | flops 269484032 | bytes 1835008 | tf_op jit(solution)/shard_map/dot_general | solution.py:8
  42.5 0.0 copy-done
  42.5 62.3 %all-gather.3.cloned.1.call-done = bf16[6144,512]{0,1:T(8,128)(2,1)} async-done(((bf16[6144,64]{0,1:T(8,128)(2,1)}), bf16[6144,512]{0,1:T(8,128)(2,1)}) %all-gather.3.cloned.1.call-update) | async-done | bytes 6291472 | tf_op jit(solution)/shard_map/all_gather | solution.py:37
  104.8 2.9 %convolution_convert_fusion.1 = bf16[6144,256]{0,1:T(8,128)(2,1)S(1)} fusion(bf16[6144,512]{0,1:T(8,128)(2,1)} %all-gather.3.cloned.1.call-done, bf16[2,256,256]{2,1,0:T(8,128)(2,1)} %param.11), kind=kOutput, calls=%fused_computation.4 | convolution fusion | flops 806879232 | bytes 6422528 | tf_op jit(solution)/shard_map/dot_general | solution.py:8
  107.7 0.0 copy-done.1
  107.7 5.5 %convolution_convert_fusion = bf16[6144,256]{0,1:T(8,128)(2,1)} fusion(bf16[6144,256]{0,1:T(8,128)(2,1)S(1)} %convolution_convert_fusion.1, bf16[256,256]{1,0:T(8,128)(2,1)S(1)} %convolution_convert_fusion.5, bf16[6144,512]{0,1:T(8,128)(2,1)} %all-gather.3.cloned.1.call-done, bf16[2,256,256]{2,1,0:T(8,128)(2,1)S(1)} %copy-done.1), kind=kOutput, calls=%fused_computation.3 | convolution fusion | flops 1616904192 | bytes 9699328 | tf_op jit(solution)/shard_map/dot_general | solution.py:8
  113.2 13.2 %subtract_convert_fusion = bf16[6144,1024]{1,0:T(8,128)(2,1)} fusion(bf16[6144,1024]{1,0:T(8,128)(2,1)} %param.6, bf16[6144,256]{0,1:T(8,128)(2,1)} %convolution_convert_fusion, bf16[6144,256]{0,1:T(8,128)(2,1)S(1)} %convolution_convert_fusion.1, bf16[256,1024]{1,0:T(8,128)(2,1)} %fusion.6, bf16[256,1024]{1,0:T(8,128)(2,1)} %copy-done), kind=kOutput, calls=%fused_computation | convolution fusion | flops 6476005376 | bytes 32505856 | tf_op jit(solution)/shard_map/dot_general | solution.py:8
Async XLA Ops:
  6.5 31.9 %all-gather.5.cloned.1.call-start = ((), (), s32[]{:S(2)}) async-start(), calls=%async_computation.1 | async-start | bytes 1310720 | tf_op jit(solution)/shard_map/all_gather | solution.py:28
  7.3 97.5 %all-gather.3.cloned.1.call-start = ((), (), s32[]{:S(2)}) async-start(), calls=%async_computation | async-start | bytes 7077888 | tf_op jit(solution)/shard_map/all_gather | solution.py:37
  10.3 97.4 %copy-start.1 = (bf16[2,256,256]{2,1,0:T(8,128)(2,1)S(1)}, bf16[2,256,256]{2,1,0:T(8,128)(2,1)}, u32[]{:S(2)}) copy-start(bf16[2,256,256]{2,1,0:T(8,128)(2,1)} %param.11) | copy-start | bytes 786436
  39.9 2.6 %copy-start = (bf16[256,1024]{1,0:T(8,128)(2,1)}, bf16[256,1024]{1,0:T(8,128)(2,1)S(1)}, u32[]{:S(2)}) copy-start(bf16[256,1024]{1,0:T(8,128)(2,1)S(1)} %convolution_convert_fusion.3) | copy-start | bytes 1572868
Sparse Core Ops, SparseCore 0:
  9.2 29.2 all-gather.4
  40.1 64.6 all-gather.2
where the time goes:
time: 133 us
  waiting for transfers between devices  91.8 us (69%)
  matrix products  27.9 us (21%)
  between operations  13.5 us (10%)
    all_gather x1, waiting for transfers between devices, on_device(): panel_full = lax.all_gather(panel_cols, 'col', axis=1, tiled=True)  62.3 us
    all_gather x1, waiting for transfers between devices, on_device(): head_full = lax.all_gather(head_slab, 'row', axis=0, tiled=True)  28.1 us
    dot_general x7, matrix products, product(): return jnp.dot(left, right, preferred_element_type=jnp.float32)  27.9 us
  transfers between devices with their start and end apart: 2, of which 2 were waited for; matrix products, arithmetic and copies ran while one was open for 5% of the time, Pallas kernels for 0%

commit v1 on v0

--- a/solution.py
+++ b/solution.py
@@ -2,6 +2,7 @@
 import jax.numpy as jnp
 from jax import lax
 from jax.sharding import PartitionSpec as P
+from jax.lax import axis_index, axis_size, ppermute
 
 
 def product(left, right):
@@ -25,7 +26,27 @@
 
 def on_device(trailing_slab, panel_cols, head_slab, coupling, lower_inverses, upper_inverses):
     width = coupling.shape[1]
-    head_full = lax.all_gather(head_slab, "row", axis=0, tiled=True)
+    small = axis_index("row")
+    arr_out = axis_size("row")
+    r_now, spare, mixed_arr = (arr_out, small, head_slab.shape[0])
+    table = [(dev, (dev + 1) % r_now) for dev in range(r_now)]
+    head_full = jnp.zeros(
+        (*head_slab.shape[:0], r_now * mixed_arr, *head_slab.shape[1:]), head_slab.dtype
+    )
+    head_full = lax.dynamic_update_slice_in_dim(head_full, head_slab, spare * mixed_arr, axis=0)
+    arrivals = [(dev, (dev - 1) % r_now) for dev in range(r_now)]
+    local_part = y2 = head_slab
+    mat_out = r_now // 2
+    for ii in [*range(1, mat_out + 1)]:
+        local_part = ppermute(local_part, "row", table)
+        head_full = lax.dynamic_update_slice_in_dim(
+            head_full, local_part, (spare - ii) % r_now * mixed_arr, axis=0
+        )
+        if ii < r_now - mat_out:
+            y2 = ppermute(y2, "row", arrivals)
+            head_full = lax.dynamic_update_slice_in_dim(
+                head_full, y2, (spare + ii) % r_now * mixed_arr, axis=0
+            )
     upper_mid = product(lower_inverses[0], coupling[0]).astype(jnp.bfloat16)
     upper_first = product(lower_inverses[0], head_full[:width]).astype(jnp.bfloat16)
     lower_head = product(coupling[1], upper_inverses[0]).astype(jnp.bfloat16)

time: 133 us -> 105 us (0.79)
  waiting for transfers between devices: 91.8 us -> 58.4 us
  starting transfers between devices: 0.04 us -> 5.11 us
    all_gather x1 -> x0, waiting for transfers between devices: 28.1 us -> none  [on_device(): head_full = lax.all_gather(head_slab, 'row', axis=0, tiled=True)]
    all_gather x1, waiting for transfers between devices: 62.3 us -> 43.4 us  [on_device(): panel_full = lax.all_gather(panel_cols, 'col', axis=1, tiled=True)]
    ppermute x0 -> x3, waiting for transfers between devices: none -> 14.2 us  [the longest x2 10.3 us: on_device(): local_part = ppermute(local_part, 'row', table)]
    ppermute x0 -> x3, starting transfers between devices: none -> 5.1 us  [the longest x2 4.08 us: on_device(): local_part = ppermute(local_part, 'row', table)]
  transfers between devices with their start and end apart: 2 -> 4, of which waited for: 2 -> 4; matrix products, arithmetic and copies ran while one was open for 5% -> 6% of each run, Pallas kernels for 0% -> 0%
where the time goes in v1:
time: 105 us
  waiting for transfers between devices  58.4 us (56%)
  matrix products  26.7 us (25%)
  between operations  13.5 us (13%)
  starting transfers between devices  5.11 us (5%)
  local copies, waits for them, and re-layouts  1.17 us (1%)
    all_gather x1, waiting for transfers between devices, on_device(): panel_full = lax.all_gather(panel_cols, 'col', axis=1, tiled=True)  43.4 us
    dot_general x7, matrix products, product(): return jnp.dot(left, right, preferred_element_type=jnp.float32)  26.7 us
    ppermute x2, waiting for transfers between devices, on_device(): local_part = ppermute(local_part, 'row', table)  10.3 us
    ppermute x2, starting transfers between devices, on_device(): local_part = ppermute(local_part, 'row', table)  4.08 us
    ppermute x1, waiting for transfers between devices, on_device(): y2 = ppermute(y2, 'row', arrivals)  3.89 us
  transfers between devices with their start and end apart: 4, of which 4 were waited for; matrix products, arithmetic and copies ran while one was open for 6% of the time, Pallas kernels for 0%

profile of v1, /device:TPU:0, one launch (start us, length us, event | category | flops | bytes accessed | tf_op | source)
XLA Modules:
  0.0 104.9 jit_solution(3216653238825906955)
XLA Ops:
  6.5 0.0 copy-start.1
  6.5 0.0 copy-start.2
  6.5 0.0 all-gather.2.cloned.1.call-start
  6.5 0.7 all-gather.2.cloned.1.call-update
  7.3 3.0 %collective-permute-start = (bf16[128,1024]{1,0:T(8,128)(2,1)}, bf16[128,1024]{1,0:T(8,128)(2,1)S(1)}, u32[]{:S(2)}, u32[]{:S(2)}) collective-permute-start(bf16[128,1024]{1,0:T(8,128)(2,1)} %param.8), channel_id=1, source_target_pairs={{0,8},{8,16},{16,24},{24,0},{1,9},{9,17},{17,25},{25,1},{2,10},{10... | collective-permute-start | bytes 786440 | tf_op jit(solution)/shard_map/ppermute | solution.py:41
  10.3 1.0 collective-permute-start.1
  11.3 1.2 %convolution_convert_fusion.5 = bf16[256,256]{1,0:T(8,128)(2,1)S(1)} fusion(bf16[2,256,256]{2,1,0:T(8,128)(2,1)} %param.9, bf16[2,256,256]{2,1,0:T(8,128)(2,1)} %param.10), kind=kOutput, calls=%fused_computation.13 | convolution fusion | flops 33619968 | bytes 393216 | tf_op jit(solution)/shard_map/dot_general | solution.py:9
  12.5 6.1 %collective-permute-done = bf16[128,1024]{1,0:T(8,128)(2,1)S(1)} collective-permute-done((bf16[128,1024]{1,0:T(8,128)(2,1)}, bf16[128,1024]{1,0:T(8,128)(2,1)S(1)}, u32[]{:S(2)}, u32[]{:S(2)}) %collective-permute-start) | collective-permute-done | bytes 262176 | tf_op jit(solution)/shard_map/ppermute | solution.py:41
  18.6 1.1 %collective-permute-start.2 = (bf16[128,1024]{1,0:T(8,128)(2,1)S(1)}, bf16[128,1024]{1,0:T(8,128)(2,1)S(1)}, u32[]{:S(2)}, u32[]{:S(2)}) collective-permute-start(bf16[128,1024]{1,0:T(8,128)(2,1)S(1)} %collective-permute-done), channel_id=1, source_target_pairs={{0,8},{8,16},{16,24},{24,0},{1,9},{9,17},{17,25},{25,1},{2,10},{10... | collective-permute-start | bytes 786440 | tf_op jit(solution)/shard_map/ppermute | solution.py:41
  19.7 0.1 broadcast_in_dim.3
  19.8 1.0 constant_dynamic-update-slice_fusion.3
  20.9 3.9 %collective-permute-done.1 = bf16[128,1024]{1,0:T(8,128)(2,1)S(1)} collective-permute-done((bf16[128,1024]{1,0:T(8,128)(2,1)}, bf16[128,1024]{1,0:T(8,128)(2,1)S(1)}, u32[]{:S(2)}, u32[]{:S(2)}) %collective-permute-start.1) | collective-permute-done | bytes 262176 | tf_op jit(solution)/shard_map/ppermute | solution.py:46
  24.8 4.2 %collective-permute-done.2 = bf16[128,1024]{1,0:T(8,128)(2,1)S(1)} collective-permute-done((bf16[128,1024]{1,0:T(8,128)(2,1)S(1)}, bf16[128,1024]{1,0:T(8,128)(2,1)S(1)}, u32[]{:S(2)}, u32[]{:S(2)}) %collective-permute-start.2) | collective-permute-done | bytes 262176 | tf_op jit(solution)/shard_map/ppermute | solution.py:41
  29.0 1.2 %convolution_convert_fusion.3 = bf16[1024,256]{0,1:T(8,128)(2,1)S(1)} fusion(bf16[512,1024]{1,0:T(8,128)(2,1)S(1)} %constant_dynamic-update-slice_fusion, bf16[2,256,256]{2,1,0:T(8,128)(2,1)} %param.10), kind=kOutput, calls=%fused_computation.10 | convolution fusion | flops 134479872 | bytes 1179648 | tf_op jit(solution)/shard_map/dot_general | solution.py:9
  30.3 0.0 copy-start
  30.3 1.6 %fusion.6 = f32[256,1024]{1,0:T(8,128)S(1)} fusion(bf16[1024,256]{0,1:T(8,128)(2,1)S(1)} %convolution_convert_fusion.3, bf16[2,256,256]{2,1,0:T(8,128)(2,1)} %param.9, bf16[2,256,256]{2,1,0:T(8,128)(2,1)} %param.11), kind=kOutput, calls=%fused_computation.14 | convolution fusion | flops 167837696 | bytes 1835008 | tf_op jit(solution)/shard_map/dot_general | solution.py:9
  31.9 0.0 copy-done.1
  31.9 1.1 %fusion.5 = bf16[256,1024]{1,0:T(8,128)(2,1)} fusion(f32[256,1024]{1,0:T(8,128)S(1)} %fusion.6, bf16[512,1024]{1,0:T(8,128)(2,1)S(1)} %constant_dynamic-update-slice_fusion, bf16[2,256,256]{2,1,0:T(8,128)(2,1)S(1)} %copy-done.1), kind=kOutput, calls=%fused_computation.11 | convolution fusion | flops 135266304 | bytes 2228224 | tf_op jit(solution)/shard_map/dot_general | solution.py:9
  33.0 0.0 copy-done
  33.0 43.4 %all-gather.2.cloned.1.call-done = bf16[6144,512]{0,1:T(8,128)(2,1)} async-done(((bf16[6144,64]{0,1:T(8,128)(2,1)}), bf16[6144,512]{0,1:T(8,128)(2,1)}) %all-gather.2.cloned.1.call-update) | async-done | bytes 6291472 | tf_op jit(solution)/shard_map/all_gather | solution.py:58
  76.4 0.0 copy-done.2
  76.4 2.9 %convolution_convert_fusion.1 = bf16[6144,256]{0,1:T(8,128)(2,1)S(1)} fusion(bf16[6144,512]{0,1:T(8,128)(2,1)} %all-gather.2.cloned.1.call-done, bf16[2,256,256]{2,1,0:T(8,128)(2,1)S(1)} %copy-done.2), kind=kOutput, calls=%fused_computation.4 | convolution fusion | flops 806879232 | bytes 6422528 | tf_op jit(solution)/shard_map/dot_general | solution.py:9
  79.3 5.5 %convolution_convert_fusion = bf16[6144,256]{0,1:T(8,128)(2,1)} fusion(bf16[6144,256]{0,1:T(8,128)(2,1)S(1)} %convolution_convert_fusion.1, bf16[256,256]{1,0:T(8,128)(2,1)S(1)} %convolution_convert_fusion.5, bf16[6144,512]{0,1:T(8,128)(2,1)} %all-gather.2.cloned.1.call-done, bf16[2,256,256]{2,1,0:T(8,128)(2,1)S(1)} %copy-done.2), kind=kOutput, calls=%fused_computation.3 | convolution fusion | flops 1616904192 | bytes 9699328 | tf_op jit(solution)/shard_map/dot_general | solution.py:9
  84.8 13.2 %subtract_convert_fusion = bf16[6144,1024]{1,0:T(8,128)(2,1)} fusion(bf16[6144,1024]{1,0:T(8,128)(2,1)} %param.6, bf16[6144,256]{0,1:T(8,128)(2,1)} %convolution_convert_fusion, bf16[6144,256]{0,1:T(8,128)(2,1)S(1)} %convolution_convert_fusion.1, bf16[256,1024]{1,0:T(8,128)(2,1)} %fusion.5, bf16[256,1024]{1,0:T(8,128)(2,1)} %bitcast.30), kind=kOutput, calls=%fused_computation | convolution fusion | flops 6476005376 | bytes 32505856 | tf_op jit(solution)/shard_map/dot_general | solution.py:9
  (3 shorter events, 0.1 us)
Async XLA Ops:
  6.5 25.3 %copy-start.1 = (bf16[2,256,256]{2,1,0:T(8,128)(2,1)S(1)}, bf16[2,256,256]{2,1,0:T(8,128)(2,1)}, u32[]{:S(2)}) copy-start(bf16[2,256,256]{2,1,0:T(8,128)(2,1)} %param.10) | copy-start | bytes 786436
  6.5 69.9 %copy-start.2 = (bf16[2,256,256]{2,1,0:T(8,128)(2,1)S(1)}, bf16[2,256,256]{2,1,0:T(8,128)(2,1)}, u32[]{:S(2)}) copy-start(bf16[2,256,256]{2,1,0:T(8,128)(2,1)} %param.11) | copy-start | bytes 786436
  6.5 69.9 %all-gather.2.cloned.1.call-start = ((), (), s32[]{:S(2)}) async-start(), calls=%async_computation | async-start | bytes 7077888 | tf_op jit(solution)/shard_map/all_gather | solution.py:58
  7.3 11.3 %collective-permute-start = (bf16[128,1024]{1,0:T(8,128)(2,1)}, bf16[128,1024]{1,0:T(8,128)(2,1)S(1)}, u32[]{:S(2)}, u32[]{:S(2)}) collective-permute-start(bf16[128,1024]{1,0:T(8,128)(2,1)} %param.8), channel_id=1, source_target_pairs={{0,8},{8,16},{16,24},{24,0},{1,9},{9,17},{17,25},{25,1},{2,10},{10... | collective-permute-start | bytes 786440 | tf_op jit(solution)/shard_map/ppermute | solution.py:41
  10.3 14.5 %collective-permute-start.1 = (bf16[128,1024]{1,0:T(8,128)(2,1)}, bf16[128,1024]{1,0:T(8,128)(2,1)S(1)}, u32[]{:S(2)}, u32[]{:S(2)}) collective-permute-start(bf16[128,1024]{1,0:T(8,128)(2,1)} %param.8), channel_id=1, source_target_pairs={{0,24},{8,0},{16,8},{24,16},{1,25},{9,1},{17,9},{25,17},{2,26},{10... | collective-permute-start | bytes 786440 | tf_op jit(solution)/shard_map/ppermute | solution.py:46
  18.6 10.4 %collective-permute-start.2 = (bf16[128,1024]{1,0:T(8,128)(2,1)S(1)}, bf16[128,1024]{1,0:T(8,128)(2,1)S(1)}, u32[]{:S(2)}, u32[]{:S(2)}) collective-permute-start(bf16[128,1024]{1,0:T(8,128)(2,1)S(1)} %collective-permute-done), channel_id=1, source_target_pairs={{0,8},{8,16},{16,24},{24,0},{1,9},{9,17},{17,25},{25,1},{2,10},{10... | collective-permute-start | bytes 786440 | tf_op jit(solution)/shard_map/ppermute | solution.py:41
  30.3 2.7 %copy-start = (bf16[1024,256]{0,1:T(8,128)(2,1)}, bf16[1024,256]{0,1:T(8,128)(2,1)S(1)}, u32[]{:S(2)}) copy-start(bf16[1024,256]{0,1:T(8,128)(2,1)S(1)} %convolution_convert_fusion.3) | copy-start | bytes 1572868
Sparse Core Ops, SparseCore 0:
  9.0 67.4 all-gather.1
